TPU v7x, 512 devices: a whole 4x4x16 slice. The times are simulated.
512 devices in a mesh: rep: 16 (over x_lo, y, core), ep: 32 (over z, x_hi).
Axes of the slice: x: 4 (x_hi: 2, x_lo: 2; x = x_hi * 2 + x_lo), y: 4, z: 16, core: 2. Of those that a mesh axis runs over, the one named last changes fastest.
Arguments:
- tokens: bfloat16 [65536, 3584], P(('rep', 'ep')), parts along dimension 0, may hold values from -6 to 6
- route_token: int32 [32768], P(('rep', 'ep')), parts along dimension 0, may hold values from 0 to 127
- route_expert: int32 [32768, 1], P(('rep', 'ep')), parts along dimension 0, may hold values from 0 to 3; in each aligned block of 64 rows (0 to 63, 64 to 127, ...) at most 24 rows name the same one
- route_gate: float32 [32768], P(('rep', 'ep')), parts along dimension 0, may hold values from 0.25 to 2.5
- w_in: bfloat16 [32, 3584, 256], P('ep'), may hold values from -0.09375 to 0.09375
- w_out: bfloat16 [32, 128, 3584], P('ep'), may hold values from -0.1875 to 0.1875
- swap_pairs: int32 [16], replicated, may hold values 0 or 1
Outputs:
- mixed: bfloat16 [65536, 3584], P(('rep', 'ep')), parts along dimension 0
- saved_hidden: bfloat16 [512, 768, 128], P(('rep', 'ep')), parts along dimension 0
There are 16 independent parts, one for each index of `rep`. A program takes and returns all parts, laid end to end along the dimension named above; an argument that names none is the same for every part. Nothing has to cross between parts.
Inputs may be any that keep to these rules, and one draw needn't show every extreme that they name: `route_expert`: in each block of 64 rows (the rows of one device) no expert is named by more than 24 rows, and some block names an expert exactly 24 times.
All inputs are finite; a program needn't handle non-finite values.
Results may differ from a plain program's by a relative error of at most 0.0057.
Values may be sent and summed in bfloat16 or wider, within the bound.
A program may use at most 64 MiB of HBM per device.

v0:
```python
import jax
import jax.numpy as jnp
from jax import lax
from jax.sharding import PartitionSpec as P

SLICES = 8


def from_behind(value, axis, steps):
    count = lax.axis_size(axis)
    pairs = [(source, (source + steps) % count) for source in range(count)]
    return lax.ppermute(value, axis, pairs)


def shards(tokens, route_token, route_expert, route_gate, w_in, w_out, swap_pairs):
    devices = lax.axis_size("ep")
    half_axis = devices // 2
    feature_width = tokens.shape[1]
    slice_units = w_out.shape[1]
    rows_dev = route_token.shape[0]
    tok_count = tokens.shape[0]
    experts = devices // SLICES
    capacity = min(rows_dev, 3 * rows_dev // (2 * experts))
    own_index = lax.axis_index("ep")
    flag_mine = swap_pairs[own_index % half_axis]
    device_ids = jnp.arange(devices, dtype=jnp.int32)
    expert_ids = route_expert[:, 0]
    expert_range = jnp.arange(experts, dtype=jnp.int32)
    expert_hits = (expert_ids[:, None] == expert_range[None, :]).astype(jnp.int32)
    slot_index = jnp.sum((jnp.cumsum(expert_hits, axis=0) - 1) * expert_hits, axis=1)
    slot_table = (expert_ids[None, None, :] == expert_range[:, None, None]) & (
        slot_index[None, None, :] == jnp.arange(capacity, dtype=jnp.int32)[None, :, None]
    )
    picked = jnp.take(tokens, route_token, axis=0)
    expert_buf = jnp.einsum(
        "ecr,rd->ecd", slot_table.astype(jnp.bfloat16), picked, preferred_element_type=jnp.float32
    ).astype(jnp.bfloat16)
    served_in = w_in[0]
    served_out = w_out[0]
    served_expert = device_ids // SLICES
    outgoing = jnp.take(expert_buf, served_expert, axis=0)
    arrived = lax.all_to_all(outgoing, "ep", split_axis=0, concat_axis=0, tiled=True)
    item_count = arrived.shape[1]
    flat_rows = arrived.reshape(-1, feature_width)
    gate_up = jnp.dot(flat_rows, served_in, preferred_element_type=jnp.float32)
    hidden = (jax.nn.silu(gate_up[:, :slice_units]) * gate_up[:, slice_units:]).astype(jnp.bfloat16)
    partial_value = jnp.dot(hidden, served_out, preferred_element_type=jnp.float32).astype(
        jnp.bfloat16
    )
    returned = lax.all_to_all(
        partial_value.reshape(devices, item_count, feature_width),
        "ep",
        split_axis=0,
        concat_axis=0,
        tiled=True,
    )
    returned, hidden_rows = (returned, hidden.reshape(devices, item_count, slice_units))
    owner_table = (served_expert[:, None] == expert_range[None, :]).astype(jnp.bfloat16)
    combined = jnp.einsum("je,jcd->ecd", owner_table, returned, preferred_element_type=jnp.float32)
    row_values = jnp.einsum(
        "ecr,ecd->rd", slot_table.astype(jnp.float32), combined, precision=lax.Precision.HIGHEST
    )
    token_table = (jnp.arange(tok_count, dtype=jnp.int32)[:, None] == route_token[None, :]).astype(
        jnp.float32
    )
    token_table = token_table * route_gate[None, :]
    mixed = jnp.dot(token_table, row_values, precision=lax.Precision.HIGHEST).astype(jnp.bfloat16)
    moved_hidden = from_behind(hidden_rows, "ep", half_axis)
    saved_rows = jnp.where(flag_mine == 1, moved_hidden, hidden_rows)
    return (mixed, saved_rows.reshape(1, devices * capacity, slice_units))


def solution(mesh):
    return jax.shard_map(
        shards,
        mesh=mesh,
        in_specs=(
            P(("rep", "ep"), None),
            P(("rep", "ep")),
            P(("rep", "ep"), None),
            P(("rep", "ep")),
            P("ep", None, None),
            P("ep", None, None),
            P(),
        ),
        out_specs=(P(("rep", "ep"), None), P(("rep", "ep"), None, None)),
        check_vma=False,
    )
```

profile of v0, /device:TPU:12, one launch (start us, length us, event | category | flops | bytes accessed | tf_op | source)
XLA Modules:
  0.0 562.1 jit_solution(12156731946267115805)
XLA Ops:
  0.6 0.0 copy-start
  0.6 0.9 fusion.14
  1.5 0.7 iota_compare_fusion.5
  2.2 0.7 compare_select_fusion.1
  2.8 0.7 compare_and_fusion
  3.5 0.1 reduce_window_sum.11
  3.6 0.8 select_reduce_fusion
  4.5 2.6 gather_fusion
  7.1 0.4 convolution_convert_fusion.2
  7.5 3.3 gather_fusion.1
  10.8 3.1 broadcast_select_fusion
  13.9 264.3 %all_to_all.10 = bf16[32,24,3584]{2,1,0:T(8,128)(2,1)S(1)} all-to-all(bf16[32,24,3584]{2,1,0:T(8,128)(2,1)S(1)} %broadcast_select_fusion), channel_id=1, replica_groups=mesh['rep'=16,'ep'=32] {'ep'}, dimensions={0} | all-to-all | bytes 11010048 | tf_op jit(solution)/shard_map/all_to_all | solution.py:42
  278.2 0.0 copy-done
  278.2 0.0 copy-start.1
  278.2 1.6 fusion.2
  279.8 0.1 fusion.9
  279.9 0.0 copy-done.1
  279.9 4.0 convolution_convert_fusion
  284.0 5.3 all-to-all-start.1
  289.2 0.0 copy-start.2
  289.3 0.0 copy-start.3
  289.3 12.1 %collective-permute-start = (bf16[32,24,128]{2,1,0:T(8,128)(2,1)S(1)}, bf16[32,24,128]{2,1,0:T(8,128)(2,1)S(1)}, u32[]{:S(2)}, u32[]{:S(2)}) collective-permute-start(bf16[32,24,128]{2,1,0:T(8,128)(2,1)S(1)} %bitcast.27), channel_id=1, source_target_pairs={{0,16},{1,17},{2,18},{3,19},{4,20},{5,21},{6,22},{7,23},{8,24},{9,... | collective-permute-start | bytes 589832 | tf_op jit(solution)/shard_map/ppermute | solution.py:12
  301.4 0.0 copy-done.4
  301.4 0.6 dynamic_slice.3
  302.6 249.4 %collective-permute-done = bf16[32,24,128]{2,1,0:T(8,128)(2,1)S(1)} collective-permute-done((bf16[32,24,128]{2,1,0:T(8,128)(2,1)S(1)}, bf16[32,24,128]{2,1,0:T(8,128)(2,1)S(1)}, u32[]{:S(2)}, u32[]{:S(2)}) %collective-permute-start) | collective-permute-done | bytes 196640 | tf_op jit(solution)/shard_map/ppermute | solution.py:12
  552.0 0.7 broadcast_select_fusion.1
  552.7 0.0 all-to-all-done.1
  552.7 5.7 %fusion = f32[4,24,3584]{2,0,1:T(4,128)S(1)} fusion(bf16[32,24,3584]{2,1,0:T(8,128)(2,1)} %all-to-all-done.1, s32[32]{0:T(128)S(1)} %and_select_fusion.1), kind=kOutput, calls=%fused_computation.3 | convolution fusion | flops 22020224 | bytes 6881408 | tf_op jit(solution)/shard_map/je,jcd->ecd/dot_general | solution.py:59
  558.5 1.1 convolution_bitcast_fusion
  559.5 0.0 copy-done.2
  559.5 0.0 copy-done.3
  559.6 2.5 convolution_convert_fusion.1
  (7 shorter events, 0.0 us)
Async XLA Ops:
  0.6 277.6 %copy-start = (bf16[1,3584,256]{2,1,0:T(8,128)(2,1)S(1)}, bf16[1,3584,256]{2,1,0:T(8,128)(2,1)}, u32[]{:S(2)}) copy-start(bf16[1,3584,256]{2,1,0:T(8,128)(2,1)} %param.11) | copy-start | bytes 5505028
  278.2 1.7 copy-start.1
  284.0 17.4 %copy-start.4 = (s32[16]{0:T(128)S(1)}, s32[16]{0:T(128)}, u32[]{:S(2)}) copy-start(s32[16]{0:T(128)} %param.13) | copy-start | bytes 196
  284.0 268.8 %all-to-all-start.1 = ((bf16[32,24,3584]{2,1,0:T(8,128)(2,1)}), bf16[32,24,3584]{2,1,0:T(8,128)(2,1)}, u32[]{:S(2)}, u32[]{:S(2)}) async-start(bf16[32,24,3584]{2,1,0:T(8,128)(2,1)} %bitcast.25), calls=%async_computation.1 | async-start | bytes 11010048 | tf_op jit(solution)/shard_map/all_to_all | solution.py:50
  289.2 270.3 %copy-start.2 = (s32[64]{0:T(128)S(1)}, s32[64]{0:T(128)}, u32[]{:S(2)}) copy-start(s32[64]{0:T(128)} %param.8) | copy-start | bytes 772
  289.3 270.3 %copy-start.3 = (f32[64]{0:T(128)S(1)}, f32[64]{0:T(128)}, u32[]{:S(2)}) copy-start(f32[64]{0:T(128)} %param.10) | copy-start | bytes 772
  289.3 262.7 %collective-permute-start = (bf16[32,24,128]{2,1,0:T(8,128)(2,1)S(1)}, bf16[32,24,128]{2,1,0:T(8,128)(2,1)S(1)}, u32[]{:S(2)}, u32[]{:S(2)}) collective-permute-start(bf16[32,24,128]{2,1,0:T(8,128)(2,1)S(1)} %bitcast.27), channel_id=1, source_target_pairs={{0,16},{1,17},{2,18},{3,19},{4,20},{5,21},{6,22},{7,23},{8,24},{9,... | collective-permute-start | bytes 589832 | tf_op jit(solution)/shard_map/ppermute | solution.py:12
where the time goes:
time: 562 us
  blocking collectives  264 us (47%)
  waiting for transfers between devices  249 us (44%)
  starting transfers between devices  17.4 us (3%)
  matrix products  15.3 us (3%)
  other arithmetic  7.77 us (1%)
  local copies, waits for them, and re-layouts  6.48 us (1%)
    all_to_all x1, blocking collectives, shards(): lax.all_to_all(outgoing, 'ep', split_axis=0, concat_axis=0, tiled=True)  264 us
    ppermute x1, waiting for transfers between devices, from_behind(): return lax.ppermute(value, axis, pairs)  249 us
    ppermute x1, starting transfers between devices, from_behind(): return lax.ppermute(value, axis, pairs)  12.1 us
  transfers between devices with their start and end apart: 2, of which 1 were waited for; matrix products, arithmetic and copies ran while one was open for 0% of the time, Pallas kernels for 0%

commit v1 on v0

v1 whole, which is shorter than its diff:
```python
import functools

import jax
import jax.numpy as jnp
from jax import lax
from jax.experimental import pallas as pl
from jax.experimental.pallas import tpu as pltpu
from jax.sharding import PartitionSpec as P

MESH = pl.DeviceIdType.MESH
BF = jnp.bfloat16
F32 = jnp.float32
CAP = 24
D = 3584
HS = 128
NO = 16
NI = 32
KI = D // NI
DH = D // 2


def loop(n, body):
    def step(i, carry):
        body(i)
        return carry

    lax.fori_loop(0, n, step, 0)


def kernel(
    tokens, tok_row, exp_row, exp_col, gate_row, swap, w_in, w_out,
    mixed, saved,
    xs, rx, pb, hs, out, ha, hb, wi, wo, gmat,
    r_send, r_recv, p_send, p_recv, h_send, ha_recv, hb_recv,
    wo_send, wo_recv, wi_send, wi_recv, co_send, co_recv, ci_send, ci_recv, loc,
):
    rep = lax.axis_index("rep")
    ep = lax.axis_index("ep")
    c = lax.rem(rep, 2)
    y = lax.rem(rep // 2, 4)
    xl = rep // 8
    xh = lax.rem(ep, 2)
    z = ep // 2
    x = 2 * xh + xl

    def dev(dx, dy, dz, dc):
        return ((lax.rem(dx, 2) * 4 + dy) * 2 + dc, dz * 2 + dx // 2)

    def plane(i):
        return lax.rem(x + i // 4, 4), lax.rem(y + lax.rem(i, 4), 4)

    ahead = lax.rem(z + 1 - 2 * c + 16, 16)
    behind = lax.rem(z - 1 + 2 * c + 16, 16)
    source = 4 * y + 2 * xl + c
    away = lax.rem((z - source) * (1 - 2 * c) + 32, 16)
    nxt = dev(x, y, ahead, c)
    mate = dev(x, y, z, 1 - c)

    barrier = pltpu.get_barrier_semaphore()

    def greet(target):
        pl.semaphore_signal(barrier, inc=1, device_id=target, device_id_type=MESH)

    def greet_plane(i):
        px, py = plane(i + 1)
        greet(dev(px, py, z, c))

    loop(15, greet_plane)
    greet(dev(x, y, behind, c))
    greet(mate)
    unit = lax.rem(z, 4)

    def greet_column(i):
        half = i // 16
        dz = lax.rem(i, 16)
        dx = 2 * xh + unit // 2
        dy = lax.rem(z + 8 * half, 16) // 4
        same = (dx == x) & (dy == y) & (dz == z)

        @pl.when(jnp.logical_not(same))
        def _():
            greet(dev(dx, dy, dz, c))

    loop(32, greet_column)
    own_a = ((unit // 2 == xl) & (z // 4 == y)).astype(jnp.int32)
    own_b = ((unit // 2 == xl) & (lax.rem(z + 8, 16) // 4 == y)).astype(jnp.int32)

    rows = exp_row.shape[1]
    earlier = (exp_col[...] == exp_row[...]) & (
        lax.broadcasted_iota(jnp.int32, (rows, rows), 0)
        < lax.broadcasted_iota(jnp.int32, (rows, rows), 1)
    )
    slot = jnp.sum(earlier.astype(F32), axis=0, keepdims=True).astype(jnp.int32)
    key = exp_row[...] * CAP + slot
    tok_hot = (lax.broadcasted_iota(jnp.int32, (128, rows), 0) == tok_row[...]).astype(F32)
    contract = (((1,), (1,)), ((), ()))
    place_all = (lax.broadcasted_iota(jnp.int32, (4 * CAP, rows), 0) == key).astype(F32)
    gmat[...] = lax.dot_general(
        tok_hot * gate_row[...], place_all, contract,
        precision=lax.Precision.HIGHEST, preferred_element_type=F32,
    )
    for e in range(4):
        place = (lax.broadcasted_iota(jnp.int32, (CAP, rows), 0) + CAP * e == key).astype(BF)
        pick = lax.dot_general(place, tok_hot.astype(BF), contract, preferred_element_type=F32).astype(BF)
        for n in range(7):
            cols = pl.ds(n * 512, 512)
            xs[e, :, cols] = jnp.dot(pick, tokens[:, cols], preferred_element_type=F32).astype(BF)

    pl.semaphore_wait(barrier, 49 - own_a - own_b)

    def wo_at(core, i):
        return wo.at[pl.ds(pl.multiple_of(128 * core + 16 * (i // 2), 16), 16), pl.ds(pl.multiple_of(DH * lax.rem(i, 2), 128), DH)]

    def wi_at(core, i):
        return wi.at[core, pl.ds(pl.multiple_of(KI * i, KI), KI)]

    def wo_src(i):
        return w_out.at[pl.ds(pl.multiple_of(16 * (i // 2), 16), 16), pl.ds(pl.multiple_of(DH * lax.rem(i, 2), 128), DH)]

    def wi_src(i):
        return w_in.at[pl.ds(pl.multiple_of(KI * i, KI), KI)]

    def remote(src, dst, send, recv, target):
        return pltpu.make_async_remote_copy(
            src_ref=src, dst_ref=dst, send_sem=send, recv_sem=recv,
            device_id=target, device_id_type=MESH,
        )

    keep_o = pltpu.make_async_copy(w_out, wo.at[pl.ds(pl.multiple_of(128 * c, 128), 128)], loc.at[0])
    keep_i = pltpu.make_async_copy(w_in, wi.at[c], loc.at[1])

    def chain_o(i, src):
        return remote(src, wo_at(c, i), wo_send.at[i], wo_recv.at[i], nxt)

    def chain_i(i, src):
        return remote(src, wi_at(c, i), wi_send.at[i], wi_recv.at[i], nxt)

    def mate_o(i, src, core):
        return remote(src, wo_at(core, i), co_send.at[i], co_recv.at[i], mate)

    def mate_i(i, src, core):
        return remote(src, wi_at(core, i), ci_send.at[i], ci_recv.at[i], mate)

    @pl.when(away == 0)
    def _():
        keep_o.start()
        keep_i.start()

        def first_o(i):
            chain_o(i, wo_src(i)).start()
            mate_o(i, wo_src(i), c).start()

        def first_i(i):
            chain_i(i, wi_src(i)).start()
            mate_i(i, wi_src(i), c).start()

        loop(NO, first_o)
        loop(NI, first_i)

    def row_copy(i):
        px, py = plane(i + 1)
        return remote(xs.at[py], rx.at[x, y], r_send.at[i], r_recv.at[i], dev(px, py, z, c))

    loop(15, lambda i: row_copy(i).start())
    mine = pltpu.make_async_copy(xs.at[y], rx.at[x, y], loc.at[2])
    mine.start()

    @pl.when(away > 0)
    def _():
        def relay_o(i):
            chain_o(i, wo_at(c, i)).wait_recv()

            @pl.when(away < 15)
            def _():
                chain_o(i, wo_at(c, i)).start()

            mate_o(i, wo_at(c, i), c).start()

        def relay_i(i):
            chain_i(i, wi_at(c, i)).wait_recv()

            @pl.when(away < 15)
            def _():
                chain_i(i, wi_at(c, i)).start()

            mate_i(i, wi_at(c, i), c).start()

        loop(NO, relay_o)
        loop(NI, relay_i)

    @pl.when(away == 0)
    def _():
        keep_o.wait()
        keep_i.wait()

    loop(NO, lambda i: mate_o(i, wo_at(1 - c, i), 1 - c).wait_recv())
    loop(NI, lambda i: mate_i(i, wi_at(1 - c, i), 1 - c).wait_recv())
    mine.wait()

    def row_arrival(i):
        px, py = lax.rem(x + 4 - (i + 1) // 4, 4), lax.rem(y + 4 - lax.rem(i + 1, 4), 4)
        remote(xs.at[py], rx.at[px, py], r_send.at[i], r_recv.at[i], dev(px, py, z, c)).wait_recv()

    loop(15, row_arrival)

    def part_copy(i):
        px, py = plane(i)
        return remote(pb.at[px, py], out.at[x, y], p_send.at[i], p_recv.at[i], dev(px, py, z, c))

    def hidden_copy(g, i):
        sx = lax.rem(x + g, 4)
        sy = i // 4
        s = lax.rem(i // 2, 2)
        half = lax.rem(i, 2)
        dz = lax.rem(4 * y + 2 * xl + s + 8 * half, 16)
        dx = 2 * xh + lax.rem(sx, 2)
        q = z * 2 + sx // 2
        same = (dx == x) & (sy == y) & (dz == z)
        src = hs.at[sx, sy, :, pl.ds(pl.multiple_of(HS * s, HS), HS)]
        return same, half, q, src, dev(dx, sy, dz, c)

    def send_hidden(g, i):
        same, half, q, src, target = hidden_copy(g, i)
        for k, (dst, recv) in enumerate(((ha, ha_recv), (hb, hb_recv))):
            @pl.when((half == k) & same)
            def _():
                pltpu.make_async_copy(src, dst.at[q], recv.at[q]).start()

            @pl.when((half == k) & jnp.logical_not(same))
            def _():
                remote(src, dst.at[q], h_send.at[g, i], recv.at[q], target).start()

    def sent_hidden(g, i):
        same, half, q, src, target = hidden_copy(g, i)

        @pl.when(jnp.logical_not(same))
        def _():
            remote(src, ha.at[q], h_send.at[g, i], ha_recv.at[q], target).wait_send()

    def group(step):
        g = lax.rem(step + 1, 4)
        sx = lax.rem(x + g, 4)
        block = rx[sx].reshape(4 * CAP, D)
        parts = []
        for s in range(2):
            gate_up = jnp.dot(block, wi[s], preferred_element_type=F32)
            v, u = gate_up[:, :HS], gate_up[:, HS:]
            parts.append((v / (1.0 + jnp.exp(-v)) * u).astype(BF))
        hidden = jnp.concatenate(parts, axis=1)
        hs[sx] = hidden.reshape(4, CAP, 2 * HS)
        for n in range(7):
            cols = pl.ds(n * 512, 512)
            partial = jnp.dot(hidden, wo[:, cols], preferred_element_type=F32).astype(BF)
            pb[sx, :, :, cols] = partial.reshape(4, CAP, 512)

        def leave(k):
            i = 4 * g + k

            @pl.when(i > 0)
            def _():
                part_copy(i).start()

        loop(4, leave)
        loop(16, lambda i: send_hidden(g, i))

    loop(4, group)
    own = pltpu.make_async_copy(pb.at[x, y], out.at[x, y], loc.at[3])
    own.start()

    def hidden_arrival(q):
        pltpu.make_async_copy(ha.at[q], ha.at[q], ha_recv.at[q]).wait()
        pltpu.make_async_copy(hb.at[q], hb.at[q], hb_recv.at[q]).wait()

    loop(32, hidden_arrival)
    flag = swap[lax.rem(ep, 16)]
    saved[...] = jnp.where(flag == 1, hb[...], ha[...])

    own.wait()

    def part_arrival(i):
        k = i + 1
        px, py = lax.rem(x + 4 - k // 4, 4), lax.rem(y + 4 - lax.rem(k, 4), 4)
        remote(pb.at[px, py], out.at[px, py], p_send.at[k], p_recv.at[k], dev(px, py, z, c)).wait_recv()

    loop(15, part_arrival)
    for n in range(7):
        cols = pl.ds(n * 512, 512)
        total = out[0, :, :, cols].astype(F32)
        for k in range(1, 4):
            total = total + out[k, :, :, cols].astype(F32)
        mixed[:, cols] = jnp.dot(
            gmat[...], total.reshape(4 * CAP, 512),
            precision=lax.Precision.HIGHEST, preferred_element_type=F32,
        ).astype(BF)

    loop(15, lambda i: row_copy(i).wait_send())
    loop(15, lambda i: part_copy(i + 1).wait_send())
    loop(64, lambda i: sent_hidden(i // 16, lax.rem(i, 16)))

    @pl.when(away < 15)
    def _():
        loop(NO, lambda i: chain_o(i, wo_at(c, i)).wait_send())
        loop(NI, lambda i: chain_i(i, wi_at(c, i)).wait_send())

    loop(NO, lambda i: mate_o(i, wo_at(c, i), c).wait_send())
    loop(NI, lambda i: mate_i(i, wi_at(c, i), c).wait_send())


def shards(tokens, route_token, route_expert, route_gate, w_in, w_out, swap_pairs):
    rows = route_token.shape[0]
    vmem = pl.BlockSpec(memory_space=pltpu.VMEM)
    hbm = pl.BlockSpec(memory_space=pl.ANY)
    dma = pltpu.SemaphoreType.DMA
    mixed, saved = pl.pallas_call(
        kernel,
        out_shape=(
            jax.ShapeDtypeStruct((128, D), BF),
            jax.ShapeDtypeStruct((32, CAP, HS), BF),
        ),
        in_specs=[vmem, vmem, vmem, vmem, vmem, pl.BlockSpec(memory_space=pltpu.SMEM), hbm, hbm],
        out_specs=(vmem, vmem),
        scratch_shapes=[
            pltpu.VMEM((4, CAP, D), BF),
            pltpu.VMEM((4, 4, CAP, D), BF),
            pltpu.VMEM((4, 4, CAP, D), BF),
            pltpu.VMEM((4, 4, CAP, 2 * HS), BF),
            pltpu.VMEM((4, 4, CAP, D), BF),
            pltpu.VMEM((32, CAP, HS), BF),
            pltpu.VMEM((32, CAP, HS), BF),
            pltpu.VMEM((2, D, 2 * HS), BF),
            pltpu.VMEM((2 * HS, D), BF),
            pltpu.VMEM((128, 4 * CAP), F32),
            dma((15,)), dma((15,)), dma((16,)), dma((16,)), dma((4, 16)), dma((32,)), dma((32,)),
            dma((NO,)), dma((NO,)), dma((NI,)), dma((NI,)), dma((NO,)), dma((NO,)), dma((NI,)), dma((NI,)),
            dma((4,)),
        ],
        compiler_params=pltpu.CompilerParams(
            collective_id=0, has_side_effects=True, vmem_limit_bytes=60 * 1024 * 1024
        ),
    )(
        tokens,
        route_token.reshape(1, rows),
        route_expert.reshape(1, rows),
        route_expert,
        route_gate.reshape(1, rows),
        swap_pairs,
        w_in[0],
        w_out[0],
    )
    return mixed, saved.reshape(1, 32 * CAP, HS)


def solution(mesh):
    return jax.shard_map(
        shards,
        mesh=mesh,
        in_specs=(
            P(("rep", "ep"), None),
            P(("rep", "ep")),
            P(("rep", "ep"), None),
            P(("rep", "ep")),
            P("ep", None, None),
            P("ep", None, None),
            P(),
        ),
        out_specs=(P(("rep", "ep"), None), P(("rep", "ep"), None, None)),
        check_vma=False,
    )
```

time: 562 us -> 174 us (0.31)
  the two profiles are of different devices: /device:TPU:12 before, /device:TPU:97 now
where the time goes in v1:
time: 174 us; the launch traced here: 173 us
  Pallas kernels  168 us (97%)
  local copies, waits for them, and re-layouts  4.24 us (2%)
    pallas_call x1, Pallas kernels, shards(): pl.pallas_call(kernel, out_shape=(jax.ShapeDtypeStruct((128, D), BF), jax...  168 us
    unnamed x5, local copies, waits for them, and re-layouts  4.24 us

profile of v1, /device:TPU:97, one launch (start us, length us, event | category | flops | bytes accessed | tf_op | source)
XLA Modules:
  0.0 173.3 jit_solution(8274113474502870462)
XLA Ops:
  0.6 1.4 copy.9.exp_col
  2.0 168.4 %shard_map.86 = (bf16[128,3584]{1,0:T(8,128)(2,1)}, bf16[32,24,128]{2,1,0:T(8,128)(2,1)}) custom-call(bf16[128,3584]{1,0:T(8,128)(2,1)} %tokens.1, s32[1,64]{1,0:T(1,128)} %bitcast.10, s32[1,64]{1,0:T(1,128)} %bitcast.9, s32[64,1]{1,0:T(8,128)} %copy.9.exp_col, f32[1,64]{1,0:T(1,128)} %bitcast.11, s32[16]{0:T(128)} %swap.1, bf16[3584,256]{1,0:T(8,128)(2,1)} %bitcast.6, ...), custom_call_target="tpu_custom_call" | custom-call | tf_op jit(solution)/shard_map/pallas_call | solution.py:314
  170.4 0.0 copy-start
  170.4 2.2 %copy.12 = bf16[128,3584]{1,0:T(8,128)(2,1)} copy(bf16[128,3584]{1,0:T(8,128)(2,1)} %get-tuple-element.8) | data formatting | bytes 1835008
  172.6 0.0 copy-done
  172.6 0.7 copy.13
Async XLA Ops:
  170.4 2.2 %copy-start = (bf16[32,24,128]{2,1,0:T(8,128)(2,1)S(1)}, bf16[32,24,128]{2,1,0:T(8,128)(2,1)}, u32[]{:S(2)}) copy-start(bf16[32,24,128]{2,1,0:T(8,128)(2,1)} %get-tuple-element.5) | copy-start | bytes 589828

commit v2 on v1

v2 whole, which is shorter than its diff:
```python
import functools

import jax
import jax.numpy as jnp
from jax import lax
from jax.experimental import pallas as pl
from jax.experimental.pallas import tpu as pltpu
from jax.sharding import PartitionSpec as P

MESH = pl.DeviceIdType.MESH
BF = jnp.bfloat16
F32 = jnp.float32
CAP = 24
D = 3584
HS = 128
DH = D // 2
NI = 14
NO = 7
NC = NI + NO
LAG = 2


def loop(n, body):
    def step(i, carry):
        body(i)
        return carry

    lax.fori_loop(0, n, step, 0)


def kernel(
    tokens, tok_row, exp_row, exp_col, gate_row, swap, w_in, w_out,
    mixed, saved,
    xs, rx, pb, hs, out, ha, hb, wt, tr, gmat,
    ry_send, ry_recv, rx_send, rx_recv, p_send, p_recv, h_send, ha_recv, hb_recv,
    m_up, m_down, m_recv, o_up, o_down, o_recv, y_send, y_recv, c_send, c_recv, seed, loc,
):
    rep = lax.axis_index("rep")
    ep = lax.axis_index("ep")
    c = lax.rem(rep, 2)
    y = lax.rem(rep // 2, 4)
    xl = rep // 8
    xh = lax.rem(ep, 2)
    z = ep // 2
    x = 2 * xh + xl

    def dev(dx, dy, dz, dc):
        return ((lax.rem(dx, 2) * 4 + dy) * 2 + dc, dz * 2 + dx // 2)

    def plane(i):
        return lax.rem(x + i // 4, 4), lax.rem(y + lax.rem(i, 4), 4)

    def swapped(v):
        return v // 2 + 2 * lax.rem(v, 2)

    expert = swapped(y)
    half = lax.rem(y, 2)
    mate = dev(x, y, z, 1 - c)
    pair = dev(x, y + 1 - 2 * half, z, c)
    above = dev(x, y, lax.rem(z + 1, 16), c)
    below = dev(x, y, lax.rem(z + 15, 16), c)
    m_at = lax.rem(z - (4 * expert + 2 * xl + c) + 32, 16)
    o_at = lax.rem(m_at + 8, 16)

    barrier = pltpu.get_barrier_semaphore()

    def greet(target):
        pl.semaphore_signal(barrier, inc=1, device_id=target, device_id_type=MESH)

    def greet_plane(i):
        px, py = plane(i + 1)
        greet(dev(px, py, z, c))

    loop(15, greet_plane)
    greet(above)
    greet(below)
    greet(mate)
    unit = lax.rem(z, 4)

    def greet_column(i):
        turn = i // 16
        dz = lax.rem(i, 16)
        dx = 2 * xh + unit // 2
        dy = swapped(lax.rem(z + 8 * turn, 16) // 4)
        same = (dx == x) & (dy == y) & (dz == z)

        @pl.when(jnp.logical_not(same))
        def _():
            greet(dev(dx, dy, dz, c))

    loop(32, greet_column)
    own_a = ((unit // 2 == xl) & (swapped(z // 4) == y)).astype(jnp.int32)
    own_b = ((unit // 2 == xl) & (swapped(lax.rem(z + 8, 16) // 4) == y)).astype(jnp.int32)

    rows = exp_row.shape[1]
    earlier = (exp_col[...] == exp_row[...]) & (
        lax.broadcasted_iota(jnp.int32, (rows, rows), 0)
        < lax.broadcasted_iota(jnp.int32, (rows, rows), 1)
    )
    slot = jnp.sum(earlier.astype(F32), axis=0, keepdims=True).astype(jnp.int32)
    line = lax.shift_right_logical(exp_row[...], 1) + 2 * (exp_row[...] & 1)
    key = line * CAP + slot
    tok_hot = (lax.broadcasted_iota(jnp.int32, (128, rows), 0) == tok_row[...]).astype(F32)
    contract = (((1,), (1,)), ((), ()))
    place_all = (lax.broadcasted_iota(jnp.int32, (4 * CAP, rows), 0) == key).astype(F32)
    gmat[...] = lax.dot_general(
        tok_hot * gate_row[...], place_all, contract,
        precision=lax.Precision.HIGHEST, preferred_element_type=F32,
    )
    for e in range(4):
        place = (lax.broadcasted_iota(jnp.int32, (CAP, rows), 0) + CAP * e == key).astype(BF)
        pick = lax.dot_general(place, tok_hot.astype(BF), contract, preferred_element_type=F32).astype(BF)
        for n in range(7):
            cols = pl.ds(n * 512, 512)
            xs[e, :, cols] = jnp.dot(pick, tokens[:, cols], preferred_element_type=F32).astype(BF)

    pl.semaphore_wait(barrier, 50 - own_a - own_b)

    def remote(src, dst, send, recv, target):
        return pltpu.make_async_remote_copy(
            src_ref=src, dst_ref=dst, send_sem=send, recv_sem=recv,
            device_id=target, device_id_type=MESH,
        )

    def y_copy(k):
        py = lax.rem(y + k + 1, 4)
        return remote(xs.at[py], rx.at[x, y], ry_send.at[k], ry_recv.at[k], dev(x, py, z, c))

    def x_copy(k, n):
        sy = lax.rem(y + 4 - k, 4)
        return remote(
            rx.at[x, sy], rx.at[x, sy], rx_send.at[k, n], rx_recv.at[k, n],
            dev(lax.rem(x + n + 1, 4), y, z, c),
        )

    def x_arrival(k, n):
        sx, sy = lax.rem(x + 3 - n, 4), lax.rem(y + 4 - k, 4)
        remote(rx.at[sx, sy], rx.at[sx, sy], rx_send.at[k, n], rx_recv.at[k, n], pair).wait_recv()

    loop(3, lambda k: y_copy(k).start())
    mine = pltpu.make_async_copy(xs.at[y], rx.at[x, y], loc.at[2])
    mine.start()

    def seed_copy(i, dst, start):
        go = lambda d: d.start() if start else d.wait()

        @pl.when(i < NI)
        def _():
            rows_at = pl.ds(pl.multiple_of(DH * half + 128 * i, 128), 128)
            go(pltpu.make_async_copy(w_in.at[rows_at], dst.at[i], seed.at[i]))

        @pl.when(i >= NI)
        def _():
            cols_at = pl.ds(pl.multiple_of(256 * (2 * (i - NI) + half), 256), 256)
            go(pltpu.make_async_copy(w_out.at[:, cols_at], dst.at[i], seed.at[i]))

    own_half = wt.at[c, half]

    @pl.when(m_at == 0)
    def _():
        loop(NC, lambda i: seed_copy(i, own_half, True))
        loop(NC, lambda i: seed_copy(i, own_half, False))

    @pl.when(o_at == 0)
    def _():
        loop(NC, lambda i: seed_copy(i, tr, True))
        loop(NC, lambda i: seed_copy(i, tr, False))

    def stream(buf, at, up, down, recv):
        far = jnp.where(at > 8, 16 - at, at)
        goes_up = at <= 7
        goes_down = (at == 0) | (at >= 10)

        def to_above(i):
            return remote(buf.at[i], buf.at[i], up.at[i], recv.at[i], above)

        def to_below(i):
            return remote(buf.at[i], buf.at[i], down.at[i], recv.at[i], below)

        def pass_on(i):
            @pl.when(at != 0)
            def _():
                to_above(i).wait_recv()

            @pl.when(goes_up)
            def _():
                to_above(i).start()

            @pl.when(goes_down)
            def _():
                to_below(i).start()

        def settle():
            @pl.when(goes_up)
            def _():
                loop(NC, lambda i: to_above(i).wait_send())

            @pl.when(goes_down)
            def _():
                loop(NC, lambda i: to_below(i).wait_send())

        return far, pass_on, settle

    m_far, m_pass, m_settle = stream(own_half, m_at, m_up, m_down, m_recv)
    o_far, o_pass, o_settle = stream(tr, o_at, o_up, o_down, o_recv)

    def pair_copy(i):
        return remote(tr.at[i], wt.at[c, half, i], y_send.at[i], y_recv.at[i], pair)

    def pair_arrival(i):
        remote(tr.at[i], wt.at[c, 1 - half, i], y_send.at[i], y_recv.at[i], pair).wait_recv()

    def mate_copy(core, h, i):
        return remote(wt.at[core, h, i], wt.at[core, h, i], c_send.at[h, i], c_recv.at[h, i], mate)

    def when_chunk(i, body):
        @pl.when((i >= 0) & (i < NC))
        def _():
            body(i)

    def tick(t):
        def on_m(i):
            m_pass(i)
            mate_copy(c, half, i).start()

        def on_o(i):
            o_pass(i)
            pair_copy(i).start()

        def on_y(i):
            pair_arrival(i)
            mate_copy(c, 1 - half, i).start()

        when_chunk(t - LAG * m_far, on_m)
        when_chunk(t - LAG * o_far, on_o)
        when_chunk(t - LAG * m_far - 3, on_y)

        @pl.when(t == 0)
        def _():
            mine.wait()
            loop(3, lambda n: x_copy(0, n).start())

        @pl.when(t == 6)
        def _():
            def second(k):
                sy = lax.rem(y + 3 - k, 4)
                remote(xs.at[sy], rx.at[x, sy], ry_send.at[k], ry_recv.at[k], pair).wait_recv()
                loop(3, lambda n: x_copy(k + 1, n).start())

            loop(3, second)

    loop(NC + 8 * LAG + 3, tick)

    def mate_arrival(i):
        mate_copy(1 - c, 0, i).wait_recv()
        mate_copy(1 - c, 1, i).wait_recv()

    loop(NC, mate_arrival)
    loop(4, lambda k: loop(3, lambda n: x_arrival(k, n)))

    def part_copy(i):
        px, py = plane(i)
        return remote(pb.at[px, py], out.at[x, y], p_send.at[i], p_recv.at[i], dev(px, py, z, c))

    def hidden_copy(g, i):
        sx = lax.rem(x + g, 4)
        sy = i // 4
        s = lax.rem(i // 2, 2)
        turn = lax.rem(i, 2)
        dz = lax.rem(4 * expert + 2 * xl + s + 8 * turn, 16)
        dx = 2 * xh + lax.rem(sx, 2)
        q = z * 2 + sx // 2
        same = (dx == x) & (sy == y) & (dz == z)
        src = hs.at[sx, sy, :, pl.ds(pl.multiple_of(HS * s, HS), HS)]
        return same, turn, q, src, dev(dx, sy, dz, c)

    def send_hidden(g, i):
        same, turn, q, src, target = hidden_copy(g, i)
        for k, (dst, recv) in enumerate(((ha, ha_recv), (hb, hb_recv))):
            @pl.when((turn == k) & same)
            def _():
                pltpu.make_async_copy(src, dst.at[q], recv.at[q]).start()

            @pl.when((turn == k) & jnp.logical_not(same))
            def _():
                remote(src, dst.at[q], h_send.at[g, i], recv.at[q], target).start()

    def sent_hidden(g, i):
        same, turn, q, src, target = hidden_copy(g, i)

        @pl.when(jnp.logical_not(same))
        def _():
            remote(src, ha.at[q], h_send.at[g, i], ha_recv.at[q], target).wait_send()

    def group(step):
        g = lax.rem(step + 1, 4)
        sx = lax.rem(x + g, 4)
        block = rx[sx].reshape(4 * CAP, D)
        parts = []
        for s in range(2):
            gate_up = jnp.dot(block[:, :DH], wt[s, 0, 0:NI].reshape(DH, 2 * HS), preferred_element_type=F32)
            gate_up += jnp.dot(block[:, DH:], wt[s, 1, 0:NI].reshape(DH, 2 * HS), preferred_element_type=F32)
            v, u = gate_up[:, :HS], gate_up[:, HS:]
            parts.append((v / (1.0 + jnp.exp(-v)) * u).astype(BF))
        hs[sx] = jnp.concatenate(parts, axis=1).reshape(4, CAP, 2 * HS)
        for n in range(14):
            partial = jnp.dot(parts[0], wt[0, n % 2, NI + n // 2], preferred_element_type=F32)
            partial += jnp.dot(parts[1], wt[1, n % 2, NI + n // 2], preferred_element_type=F32)
            pb[sx, :, :, pl.ds(n * 256, 256)] = partial.astype(BF).reshape(4, CAP, 256)

        def leave(k):
            i = 4 * g + k

            @pl.when(i > 0)
            def _():
                part_copy(i).start()

        loop(4, leave)
        loop(16, lambda i: send_hidden(g, i))

    loop(4, group)
    own = pltpu.make_async_copy(pb.at[x, y], out.at[x, y], loc.at[3])
    own.start()

    def hidden_arrival(q):
        pltpu.make_async_copy(ha.at[q], ha.at[q], ha_recv.at[q]).wait()
        pltpu.make_async_copy(hb.at[q], hb.at[q], hb_recv.at[q]).wait()

    loop(32, hidden_arrival)
    flag = swap[lax.rem(ep, 16)]
    saved[...] = jnp.where(flag == 1, hb[...], ha[...])

    own.wait()

    def part_arrival(i):
        k = i + 1
        px, py = lax.rem(x + 4 - k // 4, 4), lax.rem(y + 4 - lax.rem(k, 4), 4)
        remote(pb.at[px, py], out.at[px, py], p_send.at[k], p_recv.at[k], dev(px, py, z, c)).wait_recv()

    loop(15, part_arrival)
    for n in range(7):
        cols = pl.ds(n * 512, 512)
        total = out[0, :, :, cols].astype(F32)
        for k in range(1, 4):
            total = total + out[k, :, :, cols].astype(F32)
        mixed[:, cols] = jnp.dot(
            gmat[...], total.reshape(4 * CAP, 512),
            precision=lax.Precision.HIGHEST, preferred_element_type=F32,
        ).astype(BF)

    loop(3, lambda k: y_copy(k).wait_send())
    loop(4, lambda k: loop(3, lambda n: x_copy(k, n).wait_send()))
    loop(15, lambda i: part_copy(i + 1).wait_send())
    loop(64, lambda i: sent_hidden(i // 16, lax.rem(i, 16)))
    m_settle()
    o_settle()
    loop(NC, lambda i: pair_copy(i).wait_send())

    def mate_sent(i):
        mate_copy(c, 0, i).wait_send()
        mate_copy(c, 1, i).wait_send()

    loop(NC, mate_sent)


def shards(tokens, route_token, route_expert, route_gate, w_in, w_out, swap_pairs):
    rows = route_token.shape[0]
    vmem = pl.BlockSpec(memory_space=pltpu.VMEM)
    hbm = pl.BlockSpec(memory_space=pl.ANY)
    dma = pltpu.SemaphoreType.DMA
    mixed, saved = pl.pallas_call(
        kernel,
        out_shape=(
            jax.ShapeDtypeStruct((128, D), BF),
            jax.ShapeDtypeStruct((32, CAP, HS), BF),
        ),
        in_specs=[vmem, vmem, vmem, vmem, vmem, pl.BlockSpec(memory_space=pltpu.SMEM), hbm, hbm],
        out_specs=(vmem, vmem),
        scratch_shapes=[
            pltpu.VMEM((4, CAP, D), BF),
            pltpu.VMEM((4, 4, CAP, D), BF),
            pltpu.VMEM((4, 4, CAP, D), BF),
            pltpu.VMEM((4, 4, CAP, 2 * HS), BF),
            pltpu.VMEM((4, 4, CAP, D), BF),
            pltpu.VMEM((32, CAP, HS), BF),
            pltpu.VMEM((32, CAP, HS), BF),
            pltpu.VMEM((2, 2, NC, 128, 256), BF),
            pltpu.VMEM((NC, 128, 256), BF),
            pltpu.VMEM((128, 4 * CAP), F32),
            dma((3,)), dma((3,)), dma((4, 3)), dma((4, 3)), dma((16,)), dma((16,)), dma((4, 16)), dma((32,)), dma((32,)),
            dma((NC,)), dma((NC,)), dma((NC,)), dma((NC,)), dma((NC,)), dma((NC,)), dma((NC,)), dma((NC,)),
            dma((2, NC)), dma((2, NC)), dma((NC,)),
            dma((4,)),
        ],
        compiler_params=pltpu.CompilerParams(
            collective_id=0, has_side_effects=True, vmem_limit_bytes=60 * 1024 * 1024
        ),
    )(
        tokens,
        route_token.reshape(1, rows),
        route_expert.reshape(1, rows),
        route_expert,
        route_gate.reshape(1, rows),
        swap_pairs,
        w_in[0],
        w_out[0],
    )
    return mixed, saved.reshape(1, 32 * CAP, HS)


def solution(mesh):
    return jax.shard_map(
        shards,
        mesh=mesh,
        in_specs=(
            P(("rep", "ep"), None),
            P(("rep", "ep")),
            P(("rep", "ep"), None),
            P(("rep", "ep")),
            P("ep", None, None),
            P("ep", None, None),
            P(),
        ),
        out_specs=(P(("rep", "ep"), None), P(("rep", "ep"), None, None)),
        check_vma=False,
    )
```

time: 174 us -> 172 us (0.989)
  the two profiles are of different devices: /device:TPU:97 before, /device:TPU:35 now
where the time goes in v2:
time: 172 us
  Pallas kernels  167 us (97%)
  local copies, waits for them, and re-layouts  4.24 us (2%)
    pallas_call x1, Pallas kernels, shards(): pl.pallas_call(kernel, out_shape=(jax.ShapeDtypeStruct((128, D), BF), jax...  167 us
    unnamed x5, local copies, waits for them, and re-layouts  4.24 us

profile of v2, /device:TPU:35, one launch (start us, length us, event | category | flops | bytes accessed | tf_op | source)
XLA Modules:
  0.0 172.1 jit_solution(16230148957663326957)
XLA Ops:
  0.6 1.4 copy.9.exp_col
  2.0 167.2 %shard_map.86 = (bf16[128,3584]{1,0:T(8,128)(2,1)}, bf16[32,24,128]{2,1,0:T(8,128)(2,1)}) custom-call(bf16[128,3584]{1,0:T(8,128)(2,1)} %tokens.1, s32[1,64]{1,0:T(1,128)} %bitcast.10, s32[1,64]{1,0:T(1,128)} %bitcast.9, s32[64,1]{1,0:T(8,128)} %copy.9.exp_col, f32[1,64]{1,0:T(1,128)} %bitcast.11, s32[16]{0:T(128)} %swap.1, bf16[3584,256]{1,0:T(8,128)(2,1)} %bitcast.6, ...), custom_call_target="tpu_custom_call" | custom-call | tf_op jit(solution)/shard_map/pallas_call | solution.py:371
  169.2 0.0 copy-start
  169.2 2.2 %copy.12 = bf16[128,3584]{1,0:T(8,128)(2,1)} copy(bf16[128,3584]{1,0:T(8,128)(2,1)} %get-tuple-element.8) | data formatting | bytes 1835008
  171.4 0.0 copy-done
  171.4 0.7 copy.13
Async XLA Ops:
  169.2 2.2 %copy-start = (bf16[32,24,128]{2,1,0:T(8,128)(2,1)S(1)}, bf16[32,24,128]{2,1,0:T(8,128)(2,1)}, u32[]{:S(2)}) copy-start(bf16[32,24,128]{2,1,0:T(8,128)(2,1)} %get-tuple-element.5) | copy-start | bytes 589828

commit v3 on v2

--- a/solution.py
+++ b/solution.py
@@ -1,5 +1,3 @@
-import functools
-
 import jax
 import jax.numpy as jnp
 from jax import lax
@@ -17,7 +15,7 @@
 NI = 14
 NO = 7
 NC = NI + NO
-LAG = 2
+LAG = 3
 
 
 def loop(n, body):
@@ -31,8 +29,8 @@
 def kernel(
     tokens, tok_row, exp_row, exp_col, gate_row, swap, w_in, w_out,
     mixed, saved,
-    xs, rx, pb, hs, out, ha, hb, wt, tr, gmat,
-    ry_send, ry_recv, rx_send, rx_recv, p_send, p_recv, h_send, ha_recv, hb_recv,
+    xs, rx, pb, hs, hp, hq, rl, fa, fb, sb, out, ha, wt, tr, gmat,
+    ry_send, ry_recv, rx_send, rx_recv, l_send, l_recv, a_send, a_recv, b_send, b_recv, s_send, s_recv, h_send, h_recv, hp_send, hp_recv,
     m_up, m_down, m_recv, o_up, o_down, o_recv, y_send, y_recv, c_send, c_recv, seed, loc,
 ):
     rep = lax.axis_index("rep")
@@ -47,9 +45,6 @@
     def dev(dx, dy, dz, dc):
         return ((lax.rem(dx, 2) * 4 + dy) * 2 + dc, dz * 2 + dx // 2)
 
-    def plane(i):
-        return lax.rem(x + i // 4, 4), lax.rem(y + lax.rem(i, 4), 4)
-
     def swapped(v):
         return v // 2 + 2 * lax.rem(v, 2)
 
@@ -67,30 +62,46 @@
     def greet(target):
         pl.semaphore_signal(barrier, inc=1, device_id=target, device_id_type=MESH)
 
-    def greet_plane(i):
-        px, py = plane(i + 1)
-        greet(dev(px, py, z, c))
-
-    loop(15, greet_plane)
+    unit = lax.rem(z, 4)
+
+    def greet_column(i):
+        dx = 2 * xh + unit // 2
+        dy = swapped(z // 4)
+        same = (dx == x) & (dy == y) & (i == z)
+
+        @pl.when(jnp.logical_not(same))
+        def _():
+            greet(dev(dx, dy, i, c))
+
+    loop(16, greet_column)
+
+    def greet_rings(i):
+        greet(dev(lax.rem(x + i + 1, 4), y, z, c))
+        greet(dev(x, lax.rem(y + i + 1, 4), z, c))
+
+    loop(3, greet_rings)
     greet(above)
     greet(below)
     greet(mate)
-    unit = lax.rem(z, 4)
-
-    def greet_column(i):
-        turn = i // 16
-        dz = lax.rem(i, 16)
-        dx = 2 * xh + unit // 2
-        dy = swapped(lax.rem(z + 8 * turn, 16) // 4)
-        same = (dx == x) & (dy == y) & (dz == z)
-
-        @pl.when(jnp.logical_not(same))
-        def _():
-            greet(dev(dx, dy, dz, c))
-
-    loop(32, greet_column)
     own_a = ((unit // 2 == xl) & (swapped(z // 4) == y)).astype(jnp.int32)
-    own_b = ((unit // 2 == xl) & (swapped(lax.rem(z + 8, 16) // 4) == y)).astype(jnp.int32)
+
+    own_half = wt.at[c, half]
+
+    def seed_copy(i, dst, act):
+        @pl.when(i < NI)
+        def _():
+            rows_at = pl.ds(pl.multiple_of(DH * half + 128 * i, 128), 128)
+            act(pltpu.make_async_copy(w_in.at[rows_at], dst.at[i], seed.at[i]))
+
+        @pl.when(i >= NI)
+        def _():
+            cols_at = pl.ds(pl.multiple_of(256 * (2 * (i - NI) + half), 256), 256)
+            act(pltpu.make_async_copy(w_out.at[:, cols_at], dst.at[i], seed.at[i]))
+
+    for at, dst in ((m_at, own_half), (o_at, tr)):
+        @pl.when(at == 0)
+        def _():
+            loop(NC, lambda i: seed_copy(i, dst, lambda d: d.start()))
 
     rows = exp_row.shape[1]
     earlier = (exp_col[...] == exp_row[...]) & (
@@ -114,7 +125,7 @@
             cols = pl.ds(n * 512, 512)
             xs[e, :, cols] = jnp.dot(pick, tokens[:, cols], preferred_element_type=F32).astype(BF)
 
-    pl.semaphore_wait(barrier, 50 - own_a - own_b)
+    pl.semaphore_wait(barrier, 25 - own_a)
 
     def remote(src, dst, send, recv, target):
         return pltpu.make_async_remote_copy(
@@ -141,31 +152,6 @@
     mine = pltpu.make_async_copy(xs.at[y], rx.at[x, y], loc.at[2])
     mine.start()
 
-    def seed_copy(i, dst, start):
-        go = lambda d: d.start() if start else d.wait()
-
-        @pl.when(i < NI)
-        def _():
-            rows_at = pl.ds(pl.multiple_of(DH * half + 128 * i, 128), 128)
-            go(pltpu.make_async_copy(w_in.at[rows_at], dst.at[i], seed.at[i]))
-
-        @pl.when(i >= NI)
-        def _():
-            cols_at = pl.ds(pl.multiple_of(256 * (2 * (i - NI) + half), 256), 256)
-            go(pltpu.make_async_copy(w_out.at[:, cols_at], dst.at[i], seed.at[i]))
-
-    own_half = wt.at[c, half]
-
-    @pl.when(m_at == 0)
-    def _():
-        loop(NC, lambda i: seed_copy(i, own_half, True))
-        loop(NC, lambda i: seed_copy(i, own_half, False))
-
-    @pl.when(o_at == 0)
-    def _():
-        loop(NC, lambda i: seed_copy(i, tr, True))
-        loop(NC, lambda i: seed_copy(i, tr, False))
-
     def stream(buf, at, up, down, recv):
         far = jnp.where(at > 8, 16 - at, at)
         goes_up = at <= 7
@@ -182,6 +168,10 @@
             def _():
                 to_above(i).wait_recv()
 
+            @pl.when(at == 0)
+            def _():
+                seed_copy(i, buf, lambda d: d.wait())
+
             @pl.when(goes_up)
             def _():
                 to_above(i).start()
@@ -218,6 +208,23 @@
         def _():
             body(i)
 
+    def mate_arrival(i):
+        mate_copy(1 - c, 0, i).wait_recv()
+        mate_copy(1 - c, 1, i).wait_recv()
+
+    def activate(sx):
+        block = rx[sx].reshape(4 * CAP, D)
+        for s in range(2):
+            gate_up = jnp.dot(block[:, :DH], wt[s, 0, 0:NI].reshape(DH, 2 * HS), preferred_element_type=F32)
+            gate_up += jnp.dot(block[:, DH:], wt[s, 1, 0:NI].reshape(DH, 2 * HS), preferred_element_type=F32)
+            v, u = gate_up[:, :HS], gate_up[:, HS:]
+            act = (v / (1.0 + jnp.exp(-v)) * u).astype(BF).reshape(4, CAP, HS)
+            for sy in range(4):
+                hs[lax.rem(sx, 2), sy, s, sx // 2] = act[sy]
+
+    ready_at = jnp.maximum(LAG * m_far + NI + 6, 32)
+    hidden_swap = remote(hs, hp, hp_send.at[0], hp_recv.at[0], pair)
+
     def tick(t):
         def on_m(i):
             m_pass(i)
@@ -235,6 +242,13 @@
         when_chunk(t - LAG * o_far, on_o)
         when_chunk(t - LAG * m_far - 3, on_y)
 
+        @pl.when(t == ready_at)
+        def _():
+            loop(NI, mate_arrival)
+            loop(4, lambda k: loop(3, lambda n: x_arrival(k, n)))
+            loop(4, activate)
+            hidden_swap.start()
+
         @pl.when(t == 0)
         def _():
             mine.wait()
@@ -251,107 +265,161 @@
 
     loop(NC + 8 * LAG + 3, tick)
 
-    def mate_arrival(i):
-        mate_copy(1 - c, 0, i).wait_recv()
-        mate_copy(1 - c, 1, i).wait_recv()
-
-    loop(NC, mate_arrival)
-    loop(4, lambda k: loop(3, lambda n: x_arrival(k, n)))
-
-    def part_copy(i):
-        px, py = plane(i)
-        return remote(pb.at[px, py], out.at[x, y], p_send.at[i], p_recv.at[i], dev(px, py, z, c))
-
-    def hidden_copy(g, i):
-        sx = lax.rem(x + g, 4)
-        sy = i // 4
-        s = lax.rem(i // 2, 2)
-        turn = lax.rem(i, 2)
-        dz = lax.rem(4 * expert + 2 * xl + s + 8 * turn, 16)
-        dx = 2 * xh + lax.rem(sx, 2)
-        q = z * 2 + sx // 2
-        same = (dx == x) & (sy == y) & (dz == z)
-        src = hs.at[sx, sy, :, pl.ds(pl.multiple_of(HS * s, HS), HS)]
-        return same, turn, q, src, dev(dx, sy, dz, c)
-
-    def send_hidden(g, i):
-        same, turn, q, src, target = hidden_copy(g, i)
-        for k, (dst, recv) in enumerate(((ha, ha_recv), (hb, hb_recv))):
-            @pl.when((turn == k) & same)
-            def _():
-                pltpu.make_async_copy(src, dst.at[q], recv.at[q]).start()
-
-            @pl.when((turn == k) & jnp.logical_not(same))
-            def _():
-                remote(src, dst.at[q], h_send.at[g, i], recv.at[q], target).start()
-
-    def sent_hidden(g, i):
-        same, turn, q, src, target = hidden_copy(g, i)
+    loop(NO, lambda i: mate_arrival(NI + i))
+
+    def hidden_copy(i):
+        lo, sy, s = i // 8, lax.rem(i // 2, 4), lax.rem(i, 2)
+        dz = 4 * expert + 2 * xl + s
+        same = (lo == xl) & (sy == y) & (dz == z)
+        return same, hq.at[lo, sy, s], dev(2 * xh + lo, sy, dz, c)
+
+    kept = pl.ds(2 * z, 2)
+
+    def send_hidden(i):
+        same, src, target = hidden_copy(i)
+
+        @pl.when(same)
+        def _():
+            pltpu.make_async_copy(src, ha.at[kept], h_recv.at[z]).start()
 
         @pl.when(jnp.logical_not(same))
         def _():
-            remote(src, ha.at[q], h_send.at[g, i], ha_recv.at[q], target).wait_send()
-
-    def group(step):
-        g = lax.rem(step + 1, 4)
-        sx = lax.rem(x + g, 4)
-        block = rx[sx].reshape(4 * CAP, D)
-        parts = []
+            remote(src, ha.at[kept], h_send.at[i], h_recv.at[z], target).start()
+
+    def sent_hidden(i):
+        same, src, target = hidden_copy(i)
+
+        @pl.when(jnp.logical_not(same))
+        def _():
+            remote(src, ha.at[kept], h_send.at[i], h_recv.at[z], target).wait_send()
+
+    def match_hidden():
+        hidden_swap.wait_recv()
         for s in range(2):
-            gate_up = jnp.dot(block[:, :DH], wt[s, 0, 0:NI].reshape(DH, 2 * HS), preferred_element_type=F32)
-            gate_up += jnp.dot(block[:, DH:], wt[s, 1, 0:NI].reshape(DH, 2 * HS), preferred_element_type=F32)
-            v, u = gate_up[:, :HS], gate_up[:, HS:]
-            parts.append((v / (1.0 + jnp.exp(-v)) * u).astype(BF))
-        hs[sx] = jnp.concatenate(parts, axis=1).reshape(4, CAP, 2 * HS)
+            flag = swap[lax.rem(2 * (4 * expert + 2 * xl + s) + xh, 16)]
+            hq[:, :, s] = jnp.where(flag == 1, hp[:, :, s], hs[:, :, s])
+        loop(16, send_hidden)
+
+    ring_up = dev(lax.rem(x + 1, 4), y, z, c)
+    ring_down = dev(lax.rem(x + 3, 4), y, z, c)
+    far_x, up_x, down_x = lax.rem(x + 2, 4), lax.rem(x + 1, 4), lax.rem(x + 3, 4)
+
+    def row_of(k):
+        return lax.rem(y + k, 4)
+
+    def partials(sx):
+        parts = [
+            jnp.concatenate([hs[lax.rem(sx, 2), sy, s, sx // 2] for sy in range(4)], axis=0)
+            for s in range(2)
+        ]
         for n in range(14):
             partial = jnp.dot(parts[0], wt[0, n % 2, NI + n // 2], preferred_element_type=F32)
             partial += jnp.dot(parts[1], wt[1, n % 2, NI + n // 2], preferred_element_type=F32)
             pb[sx, :, :, pl.ds(n * 256, 256)] = partial.astype(BF).reshape(4, CAP, 256)
 
-        def leave(k):
-            i = 4 * g + k
-
-            @pl.when(i > 0)
-            def _():
-                part_copy(i).start()
-
-        loop(4, leave)
-        loop(16, lambda i: send_hidden(g, i))
-
-    loop(4, group)
-    own = pltpu.make_async_copy(pb.at[x, y], out.at[x, y], loc.at[3])
-    own.start()
+    def relay_up(k):
+        return remote(pb.at[far_x, row_of(k)], rl.at[k], l_send.at[k], l_recv.at[k], ring_up)
+
+    def relay_down(k):
+        return remote(pb.at[far_x, row_of(k)], rl.at[k], l_send.at[k], l_recv.at[k], ring_down)
+
+    def to_up(k):
+        return remote(pb.at[up_x, row_of(k)], fa.at[k], a_send.at[k], a_recv.at[k], ring_up)
+
+    def to_down(k):
+        return remote(pb.at[down_x, row_of(k)], fb.at[k], b_send.at[k], b_recv.at[k], ring_down)
+
+    def home(k):
+        return remote(sb.at[k], out.at[y], s_send.at[k], s_recv.at[k], dev(x, row_of(k), z, c))
+
+    def stage(g):
+        partials(lax.rem(x + g, 4))
+
+        @pl.when(g == 2)
+        def _():
+            relay_down(2).start()
+            relay_up(1).start()
+            relay_down(3).start()
+            relay_up(0).start()
+
+        @pl.when(g == 1)
+        def _():
+            to_up(2).start()
+            to_up(3).start()
+
+        @pl.when(g == 3)
+        def _():
+            to_down(1).start()
+            to_down(0).start()
+            match_hidden()
+
+    loop(4, lambda i: stage(jnp.where(i == 0, 2, jnp.where(i == 1, 1, jnp.where(i == 2, 3, 0)))))
+
+    def add_up(k):
+        relay_up(k).wait_recv()
+        row = row_of(k)
+        pb[up_x, row] = (pb[up_x, row].astype(F32) + rl[k].astype(F32)).astype(BF)
+        to_up(k).start()
+
+    def add_down(k):
+        relay_down(k).wait_recv()
+        row = row_of(k)
+        pb[down_x, row] = (pb[down_x, row].astype(F32) + rl[k].astype(F32)).astype(BF)
+        to_down(k).start()
+
+    def adds(i):
+        add_down(2 + i)
+        add_up(1 - i)
+
+    loop(2, adds)
+
+    def finish(i):
+        k = jnp.where(i == 0, 2, jnp.where(i == 1, 1, jnp.where(i == 2, 3, 0)))
+        to_up(k).wait_recv()
+        to_down(k).wait_recv()
+        total = pb[x, row_of(k)].astype(F32) + fa[k].astype(F32) + fb[k].astype(F32)
+
+        @pl.when(k > 0)
+        def _():
+            sb[k] = total.astype(BF)
+            home(k).start()
+
+        @pl.when(k == 0)
+        def _():
+            out[y] = total.astype(BF)
+
+    loop(4, finish)
 
     def hidden_arrival(q):
-        pltpu.make_async_copy(ha.at[q], ha.at[q], ha_recv.at[q]).wait()
-        pltpu.make_async_copy(hb.at[q], hb.at[q], hb_recv.at[q]).wait()
-
-    loop(32, hidden_arrival)
-    flag = swap[lax.rem(ep, 16)]
-    saved[...] = jnp.where(flag == 1, hb[...], ha[...])
-
-    own.wait()
-
-    def part_arrival(i):
-        k = i + 1
-        px, py = lax.rem(x + 4 - k // 4, 4), lax.rem(y + 4 - lax.rem(k, 4), 4)
-        remote(pb.at[px, py], out.at[px, py], p_send.at[k], p_recv.at[k], dev(px, py, z, c)).wait_recv()
-
-    loop(15, part_arrival)
+        pair_of = pl.ds(2 * q, 2)
+        pltpu.make_async_copy(ha.at[pair_of], ha.at[pair_of], h_recv.at[q]).wait()
+
+    loop(16, hidden_arrival)
+    saved[...] = ha[...]
+
+    def home_arrival(k):
+        remote(sb.at[k], out.at[lax.rem(y + 4 - k, 4)], s_send.at[k], s_recv.at[k], pair).wait_recv()
+
+    loop(3, lambda k: home_arrival(k + 1))
     for n in range(7):
         cols = pl.ds(n * 512, 512)
-        total = out[0, :, :, cols].astype(F32)
-        for k in range(1, 4):
-            total = total + out[k, :, :, cols].astype(F32)
         mixed[:, cols] = jnp.dot(
-            gmat[...], total.reshape(4 * CAP, 512),
+            gmat[...], out[:, :, cols].astype(F32).reshape(4 * CAP, 512),
             precision=lax.Precision.HIGHEST, preferred_element_type=F32,
         ).astype(BF)
 
     loop(3, lambda k: y_copy(k).wait_send())
     loop(4, lambda k: loop(3, lambda n: x_copy(k, n).wait_send()))
-    loop(15, lambda i: part_copy(i + 1).wait_send())
-    loop(64, lambda i: sent_hidden(i // 16, lax.rem(i, 16)))
+
+    def ring_sent(k):
+        relay_up(k).wait_send()
+        to_up(k).wait_send()
+        to_down(k).wait_send()
+
+    loop(4, ring_sent)
+    loop(3, lambda k: home(k + 1).wait_send())
+    loop(16, sent_hidden)
+    hidden_swap.wait_send()
     m_settle()
     o_settle()
     loop(NC, lambda i: pair_copy(i).wait_send())
@@ -380,14 +448,20 @@
             pltpu.VMEM((4, CAP, D), BF),
             pltpu.VMEM((4, 4, CAP, D), BF),
             pltpu.VMEM((4, 4, CAP, D), BF),
-            pltpu.VMEM((4, 4, CAP, 2 * HS), BF),
-            pltpu.VMEM((4, 4, CAP, D), BF),
-            pltpu.VMEM((32, CAP, HS), BF),
+            pltpu.VMEM((2, 4, 2, 2, CAP, HS), BF),
+            pltpu.VMEM((2, 4, 2, 2, CAP, HS), BF),
+            pltpu.VMEM((2, 4, 2, 2, CAP, HS), BF),
+            pltpu.VMEM((4, CAP, D), BF),
+            pltpu.VMEM((4, CAP, D), BF),
+            pltpu.VMEM((4, CAP, D), BF),
+            pltpu.VMEM((4, CAP, D), BF),
+            pltpu.VMEM((4, CAP, D), BF),
             pltpu.VMEM((32, CAP, HS), BF),
             pltpu.VMEM((2, 2, NC, 128, 256), BF),
             pltpu.VMEM((NC, 128, 256), BF),
             pltpu.VMEM((128, 4 * CAP), F32),
-            dma((3,)), dma((3,)), dma((4, 3)), dma((4, 3)), dma((16,)), dma((16,)), dma((4, 16)), dma((32,)), dma((32,)),
+            dma((3,)), dma((3,)), dma((4, 3)), dma((4, 3)), dma((4,)), dma((4,)), dma((4,)), dma((4,)), dma((4,)), dma((4,)), dma((4,)), dma((4,)),
+            dma((16,)), dma((16,)), dma((1,)), dma((1,)),
             dma((NC,)), dma((NC,)), dma((NC,)), dma((NC,)), dma((NC,)), dma((NC,)), dma((NC,)), dma((NC,)),
             dma((2, NC)), dma((2, NC)), dma((NC,)),
             dma((4,)),

time: 172 us -> 155 us (0.901)
  the two profiles are of different devices: /device:TPU:35 before, /device:TPU:3 now
where the time goes in v3:
time: 155 us
  Pallas kernels  150 us (97%)
  local copies, waits for them, and re-layouts  4.24 us (3%)
    pallas_call x1, Pallas kernels, shards(): pl.pallas_call(kernel, out_shape=(jax.ShapeDtypeStruct((128, D), BF), jax...  150 us
    unnamed x5, local copies, waits for them, and re-layouts  4.24 us

profile of v3, /device:TPU:3, one launch (start us, length us, event | category | flops | bytes accessed | tf_op | source)
XLA Modules:
  0.0 154.6 jit_solution(6510250873984968809)
XLA Ops:
  0.6 1.4 copy.9.exp_col
  2.0 149.7 %shard_map.86 = (bf16[128,3584]{1,0:T(8,128)(2,1)}, bf16[32,24,128]{2,1,0:T(8,128)(2,1)}) custom-call(bf16[128,3584]{1,0:T(8,128)(2,1)} %tokens.1, s32[1,64]{1,0:T(1,128)} %bitcast.10, s32[1,64]{1,0:T(1,128)} %bitcast.9, s32[64,1]{1,0:T(8,128)} %copy.9.exp_col, f32[1,64]{1,0:T(1,128)} %bitcast.11, s32[16]{0:T(128)} %swap.1, bf16[3584,256]{1,0:T(8,128)(2,1)} %bitcast.6, ...), custom_call_target="tpu_custom_call" | custom-call | tf_op jit(solution)/shard_map/pallas_call | solution.py:439
  151.7 0.0 copy-start
  151.7 2.2 %copy.12 = bf16[128,3584]{1,0:T(8,128)(2,1)} copy(bf16[128,3584]{1,0:T(8,128)(2,1)} %get-tuple-element.8) | data formatting | bytes 1835008
  153.9 0.0 copy-done
  153.9 0.7 copy.13
Async XLA Ops:
  151.7 2.2 %copy-start = (bf16[32,24,128]{2,1,0:T(8,128)(2,1)S(1)}, bf16[32,24,128]{2,1,0:T(8,128)(2,1)}, u32[]{:S(2)}) copy-start(bf16[32,24,128]{2,1,0:T(8,128)(2,1)} %get-tuple-element.5) | copy-start | bytes 589828

commit v4 on v3

--- a/solution.py
+++ b/solution.py
@@ -29,8 +29,8 @@
 def kernel(
     tokens, tok_row, exp_row, exp_col, gate_row, swap, w_in, w_out,
     mixed, saved,
-    xs, rx, pb, hs, hp, hq, rl, fa, fb, sb, out, ha, wt, tr, gmat,
-    ry_send, ry_recv, rx_send, rx_recv, l_send, l_recv, a_send, a_recv, b_send, b_recv, s_send, s_recv, h_send, h_recv, hp_send, hp_recv,
+    xs, rx, pb, hs, hp, hq, hz, rl, fa, fb, sb, out, ha, wt, tr, gmat,
+    ry_send, ry_recv, rx_send, rx_recv, l_send, l_recv, a_send, a_recv, b_send, b_recv, s_send, s_recv, g_send, g_recv, h_send, h_recv, hp_send, hp_recv,
     m_up, m_down, m_recv, o_up, o_down, o_recv, y_send, y_recv, c_send, c_recv, seed, loc,
 ):
     rep = lax.axis_index("rep")
@@ -62,28 +62,27 @@
     def greet(target):
         pl.semaphore_signal(barrier, inc=1, device_id=target, device_id_type=MESH)
 
-    unit = lax.rem(z, 4)
+    def beside(i):
+        return i // 4, lax.rem(y + i, 4)
 
     def greet_column(i):
-        dx = 2 * xh + unit // 2
-        dy = swapped(z // 4)
-        same = (dx == x) & (dy == y) & (i == z)
-
-        @pl.when(jnp.logical_not(same))
-        def _():
-            greet(dev(dx, dy, i, c))
+        @pl.when(i != z)
+        def _():
+            greet(dev(x, y, i, c))
+
+    def greet_beside(i):
+        lo, py = beside(i)
+
+        @pl.when((lo != xl) | (py != y))
+        def _():
+            greet(dev(2 * xh + lo, py, z, c))
 
     loop(16, greet_column)
-
-    def greet_rings(i):
-        greet(dev(lax.rem(x + i + 1, 4), y, z, c))
-        greet(dev(x, lax.rem(y + i + 1, 4), z, c))
-
-    loop(3, greet_rings)
+    loop(8, greet_beside)
+    loop(3, lambda i: greet(dev(lax.rem(x + i + 1, 4), y, z, c)))
     greet(above)
     greet(below)
     greet(mate)
-    own_a = ((unit // 2 == xl) & (swapped(z // 4) == y)).astype(jnp.int32)
 
     own_half = wt.at[c, half]
 
@@ -125,7 +124,7 @@
             cols = pl.ds(n * 512, 512)
             xs[e, :, cols] = jnp.dot(pick, tokens[:, cols], preferred_element_type=F32).astype(BF)
 
-    pl.semaphore_wait(barrier, 25 - own_a)
+    pl.semaphore_wait(barrier, 28)
 
     def remote(src, dst, send, recv, target):
         return pltpu.make_async_remote_copy(
@@ -225,6 +224,68 @@
     ready_at = jnp.maximum(LAG * m_far + NI + 6, 32)
     hidden_swap = remote(hs, hp, hp_send.at[0], hp_recv.at[0], pair)
 
+    first_slice = 4 * expert + 2 * xl
+
+    def spread_copy(i):
+        lo, sy = beside(i)
+        src, dst = hq.at[lo, sy], hz.at[pl.ds(first_slice, 2)]
+        return (lo == xl) & (sy == y), src, dst, dev(2 * xh + lo, sy, z, c)
+
+    def spread_hidden(i):
+        same, src, dst, target = spread_copy(i)
+
+        @pl.when(same)
+        def _():
+            pltpu.make_async_copy(src, dst, g_recv.at[first_slice // 2]).start()
+
+        @pl.when(jnp.logical_not(same))
+        def _():
+            remote(src, dst, g_send.at[i], g_recv.at[first_slice // 2], target).start()
+
+    def spread_sent(i):
+        same, src, dst, target = spread_copy(i)
+
+        @pl.when(jnp.logical_not(same))
+        def _():
+            remote(src, dst, g_send.at[i], g_recv.at[first_slice // 2], target).wait_send()
+
+    kept = pl.ds(2 * z, 2)
+
+    def column_copy(i):
+        return remote(hz.at[i], ha.at[kept], h_send.at[i], h_recv.at[z], dev(x, y, i, c))
+
+    def send_column(i):
+        @pl.when(i == z)
+        def _():
+            pltpu.make_async_copy(hz.at[i], ha.at[kept], h_recv.at[z]).start()
+
+        @pl.when(i != z)
+        def _():
+            column_copy(i).start()
+
+    def column_sent(i):
+        @pl.when(i != z)
+        def _():
+            column_copy(i).wait_send()
+
+    def forward_hidden():
+        def both(n):
+            piece = hz.at[pl.ds(2 * n, 2)]
+            pltpu.make_async_copy(piece, piece, g_recv.at[n]).wait()
+            send_column(2 * n)
+            send_column(2 * n + 1)
+
+        loop(8, both)
+
+    def match_hidden():
+        hidden_swap.wait_recv()
+        for s in range(2):
+            flag = swap[lax.rem(2 * (first_slice + s) + xh, 16)]
+            hq[:, :, s] = jnp.where(flag == 1, hp[:, :, s], hs[:, :, s])
+        loop(8, spread_hidden)
+
+    match_at = jnp.maximum(LAG * jnp.maximum(m_far, o_far) + NI + 6, 32) + 3
+
     def tick(t):
         def on_m(i):
             m_pass(i)
@@ -249,6 +310,10 @@
             loop(4, activate)
             hidden_swap.start()
 
+        @pl.when(t == match_at)
+        def _():
+            match_hidden()
+
         @pl.when(t == 0)
         def _():
             mine.wait()
@@ -266,39 +331,6 @@
     loop(NC + 8 * LAG + 3, tick)
 
     loop(NO, lambda i: mate_arrival(NI + i))
-
-    def hidden_copy(i):
-        lo, sy, s = i // 8, lax.rem(i // 2, 4), lax.rem(i, 2)
-        dz = 4 * expert + 2 * xl + s
-        same = (lo == xl) & (sy == y) & (dz == z)
-        return same, hq.at[lo, sy, s], dev(2 * xh + lo, sy, dz, c)
-
-    kept = pl.ds(2 * z, 2)
-
-    def send_hidden(i):
-        same, src, target = hidden_copy(i)
-
-        @pl.when(same)
-        def _():
-            pltpu.make_async_copy(src, ha.at[kept], h_recv.at[z]).start()
-
-        @pl.when(jnp.logical_not(same))
-        def _():
-            remote(src, ha.at[kept], h_send.at[i], h_recv.at[z], target).start()
-
-    def sent_hidden(i):
-        same, src, target = hidden_copy(i)
-
-        @pl.when(jnp.logical_not(same))
-        def _():
-            remote(src, ha.at[kept], h_send.at[i], h_recv.at[z], target).wait_send()
-
-    def match_hidden():
-        hidden_swap.wait_recv()
-        for s in range(2):
-            flag = swap[lax.rem(2 * (4 * expert + 2 * xl + s) + xh, 16)]
-            hq[:, :, s] = jnp.where(flag == 1, hp[:, :, s], hs[:, :, s])
-        loop(16, send_hidden)
 
     ring_up = dev(lax.rem(x + 1, 4), y, z, c)
     ring_down = dev(lax.rem(x + 3, 4), y, z, c)
@@ -351,7 +383,7 @@
         def _():
             to_down(1).start()
             to_down(0).start()
-            match_hidden()
+            forward_hidden()
 
     loop(4, lambda i: stage(jnp.where(i == 0, 2, jnp.where(i == 1, 1, jnp.where(i == 2, 3, 0)))))
 
@@ -418,7 +450,8 @@
 
     loop(4, ring_sent)
     loop(3, lambda k: home(k + 1).wait_send())
-    loop(16, sent_hidden)
+    loop(8, spread_sent)
+    loop(16, column_sent)
     hidden_swap.wait_send()
     m_settle()
     o_settle()
@@ -451,6 +484,7 @@
             pltpu.VMEM((2, 4, 2, 2, CAP, HS), BF),
             pltpu.VMEM((2, 4, 2, 2, CAP, HS), BF),
             pltpu.VMEM((2, 4, 2, 2, CAP, HS), BF),
+            pltpu.VMEM((16, 2, CAP, HS), BF),
             pltpu.VMEM((4, CAP, D), BF),
             pltpu.VMEM((4, CAP, D), BF),
             pltpu.VMEM((4, CAP, D), BF),
@@ -461,7 +495,7 @@
             pltpu.VMEM((NC, 128, 256), BF),
             pltpu.VMEM((128, 4 * CAP), F32),
             dma((3,)), dma((3,)), dma((4, 3)), dma((4, 3)), dma((4,)), dma((4,)), dma((4,)), dma((4,)), dma((4,)), dma((4,)), dma((4,)), dma((4,)),
-            dma((16,)), dma((16,)), dma((1,)), dma((1,)),
+            dma((8,)), dma((8,)), dma((16,)), dma((16,)), dma((1,)), dma((1,)),
             dma((NC,)), dma((NC,)), dma((NC,)), dma((NC,)), dma((NC,)), dma((NC,)), dma((NC,)), dma((NC,)),
             dma((2, NC)), dma((2, NC)), dma((NC,)),
             dma((4,)),

time: 155 us -> 136 us (0.88)
  the two profiles are of different devices: /device:TPU:3 before, /device:TPU:43 now
where the time goes in v4:
time: 136 us
  Pallas kernels  131 us (96%)
  local copies, waits for them, and re-layouts  4.24 us (3%)
    pallas_call x1, Pallas kernels, shards(): pl.pallas_call(kernel, out_shape=(jax.ShapeDtypeStruct((128, D), BF), jax...  131 us
    unnamed x5, local copies, waits for them, and re-layouts  4.24 us

profile of v4, /device:TPU:43, one launch (start us, length us, event | category | flops | bytes accessed | tf_op | source)
XLA Modules:
  0.0 135.8 jit_solution(15160378590263691550)
XLA Ops:
  0.6 1.4 %copy.9.exp_col = s32[64,1]{1,0:T(8,128)} copy(s32[64,1]{0,1:T(1,128)} %param.9) | data formatting | bytes 512 | tf_op args[2]
  2.0 130.9 %shard_map.86 = (bf16[128,3584]{1,0:T(8,128)(2,1)}, bf16[32,24,128]{2,1,0:T(8,128)(2,1)}) custom-call(bf16[128,3584]{1,0:T(8,128)(2,1)} %tokens.1, s32[1,64]{1,0:T(1,128)} %bitcast.10, s32[1,64]{1,0:T(1,128)} %bitcast.9, s32[64,1]{1,0:T(8,128)} %copy.9.exp_col, f32[1,64]{1,0:T(1,128)} %bitcast.11, s32[16]{0:T(128)} %swap.1, bf16[3584,256]{1,0:T(8,128)(2,1)} %bitcast.6, ...), custom_call_target="tpu_custom_call" | custom-call | tf_op jit(solution)/shard_map/pallas_call | solution.py:472
  132.9 0.0 copy-start
  132.9 2.2 %copy.12 = bf16[128,3584]{1,0:T(8,128)(2,1)} copy(bf16[128,3584]{1,0:T(8,128)(2,1)} %get-tuple-element.8) | data formatting | bytes 1835008
  135.1 0.0 copy-done
  135.1 0.7 copy.13
Async XLA Ops:
  132.9 2.2 %copy-start = (bf16[32,24,128]{2,1,0:T(8,128)(2,1)S(1)}, bf16[32,24,128]{2,1,0:T(8,128)(2,1)}, u32[]{:S(2)}) copy-start(bf16[32,24,128]{2,1,0:T(8,128)(2,1)} %get-tuple-element.5) | copy-start | bytes 589828

commit v5 on v4

--- a/solution.py
+++ b/solution.py
@@ -15,7 +15,7 @@
 NI = 14
 NO = 7
 NC = NI + NO
-LAG = 3
+LAG = 2
 
 
 def loop(n, body):
@@ -113,10 +113,13 @@
     tok_hot = (lax.broadcasted_iota(jnp.int32, (128, rows), 0) == tok_row[...]).astype(F32)
     contract = (((1,), (1,)), ((), ()))
     place_all = (lax.broadcasted_iota(jnp.int32, (4 * CAP, rows), 0) == key).astype(F32)
-    gmat[...] = lax.dot_general(
+    gates = lax.dot_general(
         tok_hot * gate_row[...], place_all, contract,
         precision=lax.Precision.HIGHEST, preferred_element_type=F32,
     )
+    for n in range(3):
+        gmat[n] = gates.astype(BF)
+        gates = gates - gmat[n].astype(F32)
     for e in range(4):
         place = (lax.broadcasted_iota(jnp.int32, (CAP, rows), 0) + CAP * e == key).astype(BF)
         pick = lax.dot_general(place, tok_hot.astype(BF), contract, preferred_element_type=F32).astype(BF)
@@ -199,8 +202,14 @@
     def pair_arrival(i):
         remote(tr.at[i], wt.at[c, 1 - half, i], y_send.at[i], y_recv.at[i], pair).wait_recv()
 
-    def mate_copy(core, h, i):
-        return remote(wt.at[core, h, i], wt.at[core, h, i], c_send.at[h, i], c_recv.at[h, i], mate)
+    def mate_copy(core, h, j):
+        part = wt.at[core, h, pl.ds(NO * j, NO)]
+        return remote(part, part, c_send.at[h, j], c_recv.at[h, j], mate)
+
+    def to_mate(h, i):
+        @pl.when(lax.rem(i, NO) == NO - 1)
+        def _():
+            mate_copy(c, h, i // NO).start()
 
     def when_chunk(i, body):
         @pl.when((i >= 0) & (i < NC))
@@ -289,7 +298,7 @@
     def tick(t):
         def on_m(i):
             m_pass(i)
-            mate_copy(c, half, i).start()
+            to_mate(half, i)
 
         def on_o(i):
             o_pass(i)
@@ -297,7 +306,7 @@
 
         def on_y(i):
             pair_arrival(i)
-            mate_copy(c, 1 - half, i).start()
+            to_mate(1 - half, i)
 
         when_chunk(t - LAG * m_far, on_m)
         when_chunk(t - LAG * o_far, on_o)
@@ -305,7 +314,7 @@
 
         @pl.when(t == ready_at)
         def _():
-            loop(NI, mate_arrival)
+            loop(NI // NO, mate_arrival)
             loop(4, lambda k: loop(3, lambda n: x_arrival(k, n)))
             loop(4, activate)
             hidden_swap.start()
@@ -319,7 +328,7 @@
             mine.wait()
             loop(3, lambda n: x_copy(0, n).start())
 
-        @pl.when(t == 6)
+        @pl.when(t == jnp.where((m_at == 0) | (o_at == 0), NC + 1, 10))
         def _():
             def second(k):
                 sy = lax.rem(y + 3 - k, 4)
@@ -330,7 +339,7 @@
 
     loop(NC + 8 * LAG + 3, tick)
 
-    loop(NO, lambda i: mate_arrival(NI + i))
+    mate_arrival(NI // NO)
 
     ring_up = dev(lax.rem(x + 1, 4), y, z, c)
     ring_down = dev(lax.rem(x + 3, 4), y, z, c)
@@ -387,6 +396,18 @@
 
     loop(4, lambda i: stage(jnp.where(i == 0, 2, jnp.where(i == 1, 1, jnp.where(i == 2, 3, 0)))))
 
+    loop(3, lambda k: y_copy(k).wait_send())
+    loop(4, lambda k: loop(3, lambda n: x_copy(k, n).wait_send()))
+    m_settle()
+    o_settle()
+    loop(NC, lambda i: pair_copy(i).wait_send())
+
+    def mate_sent(i):
+        mate_copy(c, 0, i).wait_send()
+        mate_copy(c, 1, i).wait_send()
+
+    loop(NC // NO, mate_sent)
+
     def add_up(k):
         relay_up(k).wait_recv()
         row = row_of(k)
@@ -435,13 +456,11 @@
     loop(3, lambda k: home_arrival(k + 1))
     for n in range(7):
         cols = pl.ds(n * 512, 512)
-        mixed[:, cols] = jnp.dot(
-            gmat[...], out[:, :, cols].astype(F32).reshape(4 * CAP, 512),
-            precision=lax.Precision.HIGHEST, preferred_element_type=F32,
+        rows_out = out[:, :, cols].astype(F32).reshape(4 * CAP, 512).astype(BF)
+        mixed[:, cols] = sum(
+            jnp.dot(gmat[m], rows_out, preferred_element_type=F32) for m in (2, 1, 0)
         ).astype(BF)
 
-    loop(3, lambda k: y_copy(k).wait_send())
-    loop(4, lambda k: loop(3, lambda n: x_copy(k, n).wait_send()))
 
     def ring_sent(k):
         relay_up(k).wait_send()
@@ -453,15 +472,6 @@
     loop(8, spread_sent)
     loop(16, column_sent)
     hidden_swap.wait_send()
-    m_settle()
-    o_settle()
-    loop(NC, lambda i: pair_copy(i).wait_send())
-
-    def mate_sent(i):
-        mate_copy(c, 0, i).wait_send()
-        mate_copy(c, 1, i).wait_send()
-
-    loop(NC, mate_sent)
 
 
 def shards(tokens, route_token, route_expert, route_gate, w_in, w_out, swap_pairs):
@@ -493,11 +503,11 @@
             pltpu.VMEM((32, CAP, HS), BF),
             pltpu.VMEM((2, 2, NC, 128, 256), BF),
             pltpu.VMEM((NC, 128, 256), BF),
-            pltpu.VMEM((128, 4 * CAP), F32),
+            pltpu.VMEM((3, 128, 4 * CAP), BF),
             dma((3,)), dma((3,)), dma((4, 3)), dma((4, 3)), dma((4,)), dma((4,)), dma((4,)), dma((4,)), dma((4,)), dma((4,)), dma((4,)), dma((4,)),
             dma((8,)), dma((8,)), dma((16,)), dma((16,)), dma((1,)), dma((1,)),
             dma((NC,)), dma((NC,)), dma((NC,)), dma((NC,)), dma((NC,)), dma((NC,)), dma((NC,)), dma((NC,)),
-            dma((2, NC)), dma((2, NC)), dma((NC,)),
+            dma((2, NC // NO)), dma((2, NC // NO)), dma((NC,)),
             dma((4,)),
         ],
         compiler_params=pltpu.CompilerParams(

time: 136 us -> 132 us (0.971)
  the two profiles are of different devices: /device:TPU:43 before, /device:TPU:3 now
where the time goes in v5:
time: 132 us
  Pallas kernels  127 us (96%)
  local copies, waits for them, and re-layouts  4.24 us (3%)
    pallas_call x1, Pallas kernels, shards(): pl.pallas_call(kernel, out_shape=(jax.ShapeDtypeStruct((128, D), BF), jax...  127 us
    unnamed x5, local copies, waits for them, and re-layouts  4.24 us

profile of v5, /device:TPU:3, one launch (start us, length us, event | category | flops | bytes accessed | tf_op | source)
XLA Modules:
  0.0 132.1 jit_solution(5134941142984406406)
XLA Ops:
  0.6 1.4 %copy.9.exp_col = s32[64,1]{1,0:T(8,128)} copy(s32[64,1]{0,1:T(1,128)} %param.9) | data formatting | bytes 512 | tf_op args[2]
  2.0 127.3 %shard_map.86 = (bf16[128,3584]{1,0:T(8,128)(2,1)}, bf16[32,24,128]{2,1,0:T(8,128)(2,1)}) custom-call(bf16[128,3584]{1,0:T(8,128)(2,1)} %tokens.1, s32[1,64]{1,0:T(1,128)} %bitcast.10, s32[1,64]{1,0:T(1,128)} %bitcast.9, s32[64,1]{1,0:T(8,128)} %copy.9.exp_col, f32[1,64]{1,0:T(1,128)} %bitcast.11, s32[16]{0:T(128)} %swap.1, bf16[3584,256]{1,0:T(8,128)(2,1)} %bitcast.6, ...), custom_call_target="tpu_custom_call" | custom-call | tf_op jit(solution)/shard_map/pallas_call | solution.py:482
  129.3 0.0 copy-start
  129.3 2.2 %copy.12 = bf16[128,3584]{1,0:T(8,128)(2,1)} copy(bf16[128,3584]{1,0:T(8,128)(2,1)} %get-tuple-element.8) | data formatting | bytes 1835008
  131.5 0.0 copy-done
  131.5 0.7 copy.13
Async XLA Ops:
  129.3 2.2 %copy-start = (bf16[32,24,128]{2,1,0:T(8,128)(2,1)S(1)}, bf16[32,24,128]{2,1,0:T(8,128)(2,1)}, u32[]{:S(2)}) copy-start(bf16[32,24,128]{2,1,0:T(8,128)(2,1)} %get-tuple-element.5) | copy-start | bytes 589828

commit v6 on v5

--- a/solution.py
+++ b/solution.py
@@ -27,7 +27,7 @@
 
 
 def kernel(
-    tokens, tok_row, exp_row, exp_col, gate_row, swap, w_in, w_out,
+    tokens, tok_row, exp_row, gate_row, swap, w_in, w_out,
     mixed, saved,
     xs, rx, pb, hs, hp, hq, hz, rl, fa, fb, sb, out, ha, wt, tr, gmat,
     ry_send, ry_recv, rx_send, rx_recv, l_send, l_recv, a_send, a_recv, b_send, b_recv, s_send, s_recv, g_send, g_recv, h_send, h_recv, hp_send, hp_recv,
@@ -103,11 +103,13 @@
             loop(NC, lambda i: seed_copy(i, dst, lambda d: d.start()))
 
     rows = exp_row.shape[1]
-    earlier = (exp_col[...] == exp_row[...]) & (
+    earlier = (
         lax.broadcasted_iota(jnp.int32, (rows, rows), 0)
         < lax.broadcasted_iota(jnp.int32, (rows, rows), 1)
-    )
-    slot = jnp.sum(earlier.astype(F32), axis=0, keepdims=True).astype(jnp.int32)
+    ).astype(F32)
+    hits = (lax.broadcasted_iota(jnp.int32, (8, rows), 0) == exp_row[...]).astype(F32)
+    counts = jnp.dot(hits, earlier, preferred_element_type=F32)
+    slot = jnp.sum(hits * counts, axis=0, keepdims=True).astype(jnp.int32)
     line = lax.shift_right_logical(exp_row[...], 1) + 2 * (exp_row[...] & 1)
     key = line * CAP + slot
     tok_hot = (lax.broadcasted_iota(jnp.int32, (128, rows), 0) == tok_row[...]).astype(F32)
@@ -485,7 +487,7 @@
             jax.ShapeDtypeStruct((128, D), BF),
             jax.ShapeDtypeStruct((32, CAP, HS), BF),
         ),
-        in_specs=[vmem, vmem, vmem, vmem, vmem, pl.BlockSpec(memory_space=pltpu.SMEM), hbm, hbm],
+        in_specs=[vmem, vmem, vmem, vmem, pl.BlockSpec(memory_space=pltpu.SMEM), hbm, hbm],
         out_specs=(vmem, vmem),
         scratch_shapes=[
             pltpu.VMEM((4, CAP, D), BF),
@@ -517,7 +519,6 @@
         tokens,
         route_token.reshape(1, rows),
         route_expert.reshape(1, rows),
-        route_expert,
         route_gate.reshape(1, rows),
         swap_pairs,
         w_in[0],

time: 132 us -> 131 us (level)
  local copies, waits for them, and re-layouts: 4.24 us -> 2.88 us
    unnamed x5 -> x4, local copies, waits for them, and re-layouts: 4.24 us -> 2.88 us
where the time goes in v6:
time: 131 us
  Pallas kernels  127 us (97%)
  local copies, waits for them, and re-layouts  2.88 us (2%)
    pallas_call x1, Pallas kernels, shards(): pl.pallas_call(kernel, out_shape=(jax.ShapeDtypeStruct((128, D), BF), jax...  127 us
    unnamed x4, local copies, waits for them, and re-layouts  2.88 us

profile of v6, /device:TPU:3, one launch (start us, length us, event | category | flops | bytes accessed | tf_op | source)
XLA Modules:
  0.0 130.8 jit_solution(1101929104680901182)
XLA Ops:
  0.6 127.3 %shard_map.86 = (bf16[128,3584]{1,0:T(8,128)(2,1)}, bf16[32,24,128]{2,1,0:T(8,128)(2,1)}) custom-call(bf16[128,3584]{1,0:T(8,128)(2,1)} %tokens.1, s32[1,64]{1,0:T(1,128)} %bitcast.9, s32[1,64]{1,0:T(1,128)} %bitcast.10, f32[1,64]{1,0:T(1,128)} %bitcast.11, s32[16]{0:T(128)} %swap.1, bf16[3584,256]{1,0:T(8,128)(2,1)} %bitcast.6, bf16[128,3584]{1,0:T(8,128)(2,1)} %bitcast.7), custom_call_target="tpu_custom_call" | custom-call | tf_op jit(solution)/shard_map/pallas_call | solution.py:484
  127.9 0.0 copy-start
  127.9 2.2 %copy.11 = bf16[128,3584]{1,0:T(8,128)(2,1)} copy(bf16[128,3584]{1,0:T(8,128)(2,1)} %get-tuple-element.8) | data formatting | bytes 1835008
  130.1 0.0 copy-done
  130.1 0.7 copy.12
Async XLA Ops:
  127.9 2.2 %copy-start = (bf16[32,24,128]{2,1,0:T(8,128)(2,1)S(1)}, bf16[32,24,128]{2,1,0:T(8,128)(2,1)}, u32[]{:S(2)}) copy-start(bf16[32,24,128]{2,1,0:T(8,128)(2,1)} %get-tuple-element.5) | copy-start | bytes 589828
